TPU v7x, 32 devices: a whole 2x2x4 slice. The times are simulated.
32 devices in a mesh: seq: 8 (over y, x, core), exp: 4 (over z).
Axes of the slice: x: 2, y: 2, z: 4, core: 2. Of those that a mesh axis runs over, the one named last changes fastest.
Arguments:
- queries: bfloat16 [1024, 2048], P('seq', 'exp'), may hold values from -10 to 10
- key_rows: bfloat16 [1024, 2048], P('seq', 'exp'), may hold values from -10 to 10
- value_rows: bfloat16 [1024, 2048], P('seq', 'exp'), may hold values from -6 to 6
- residual: bfloat16 [1024, 2048], P('seq'), may hold values from -20 to 20
- out_weight: bfloat16 [2048, 2048], P('exp'), may hold values from -1 to 1
- norm_gain: float32 [2048], replicated, may hold values from 0.5 to 1.5
- gate_weight: bfloat16 [16, 2048, 1408], P('seq', None, 'exp'), may hold values from -0.125 to 0.125
- up_weight: bfloat16 [16, 2048, 1408], P('seq', None, 'exp'), may hold values from -0.125 to 0.125
- down_weight: bfloat16 [16, 1408, 2048], P('seq', 'exp'), may hold values from -0.15625 to 0.15625
- routes: int32 [1024, 6], P('seq'), may hold values from 0 to 15, all different within a row; in each aligned block of 128 rows (0 to 127, 128 to 255, ...) at most 96 rows name the same one
- route_gates: float32 [1024, 6], P('seq'), may hold values from 0.2 to 1
- block_picks: int32 [2, 3], replicated, may hold values from 0 to 1, as said below
Outputs:
- layer_out: bfloat16 [1024, 2048], P(('seq', 'exp'))
Inputs may be any that keep to these rules, and one draw needn't show every extreme that they name: `block_picks`: row b names block b first, then blocks at or before b, repeats allowed. `routes`: in each aligned block of 128 rows no expert is named by more than 96 rows, a bound that some block reaches.
All inputs are finite; a program needn't handle non-finite values.
Results may differ from a plain program's by a relative error of at most 0.015.
Values may be sent and summed in bfloat16 or wider, within the bound.
No kernel may reach another device: no remote copies, remote signals or barrier semaphores. Data moves between devices by JAX's collectives and lax.ppermute only.
A program may use at most 64 MiB of HBM per device.

v0:
```python
import jax
import jax.numpy as jnp
from jax import lax
from jax.sharding import PartitionSpec as P

HD = 128
TOPK = 6
BLK = 512


def rms_scale(hidden, norm_gain):
    mean_square = jnp.mean(hidden * hidden, axis=-1, keepdims=True)
    return hidden * lax.rsqrt(mean_square + 1e-06) * norm_gain


def expert_block(arrived, gate_weight, up_weight, down_weight):
    gate_part = jnp.einsum(
        "semd,edf->semf", arrived, gate_weight, preferred_element_type=jnp.float32
    )
    up_part = jnp.einsum("semd,edf->semf", arrived, up_weight, preferred_element_type=jnp.float32)
    inner_act = (jax.nn.silu(gate_part) * up_part).astype(jnp.bfloat16)
    return jnp.einsum(
        "semf,efd->semd", inner_act, down_weight, preferred_element_type=jnp.float32
    ).astype(jnp.bfloat16)


def per_device(
    queries,
    key_rows,
    value_rows,
    residual,
    out_weight,
    norm_gain,
    gate_weight,
    up_weight,
    down_weight,
    routes,
    route_gates,
    block_picks,
):
    seq_count = lax.axis_size("seq")
    exp_count = lax.axis_size("exp")
    seq_index = lax.axis_index("seq")
    exp_index = lax.axis_index("exp")
    tok_rows = queries.shape[0]
    head_count = queries.shape[1] // HD
    nblocks = block_picks.shape[0]
    model_width = residual.shape[1]
    positions = seq_index * tok_rows + jnp.arange(tok_rows, dtype=jnp.int32)
    block_ids = jnp.arange(nblocks, dtype=jnp.int32)
    chosen = jnp.any(block_picks[:, :, None] == block_ids[None, None, :], axis=1).astype(
        jnp.float32
    )
    query_onehot = ((positions // BLK)[:, None] == block_ids[None, :]).astype(jnp.float32)
    query_allowed = jnp.dot(query_onehot, chosen)
    split_queries = queries.reshape(tok_rows, head_count, HD)
    score_scale = HD ** (-0.5)
    run_max = jnp.full((tok_rows, head_count), -1e30, jnp.float32)
    key_piece = lax.all_gather(key_rows, "seq", axis=0, tiled=True)
    value_piece = lax.all_gather(value_rows, "seq", axis=0, tiled=True)
    piece_rows = key_piece.shape[0]
    key_pos = jnp.arange(piece_rows, dtype=jnp.int32)
    key_onehot = ((key_pos // BLK)[:, None] == block_ids[None, :]).astype(jnp.float32)
    allowed = (
        (jnp.dot(query_allowed, key_onehot.T) > 0.5) & (key_pos[None, :] <= positions[:, None])
    )[:, None, :]
    scores = (
        jnp.einsum(
            "qhd,khd->qhk",
            split_queries,
            key_piece.reshape(piece_rows, head_count, HD),
            preferred_element_type=jnp.float32,
        )
        * score_scale
    )
    piece_max = jnp.max(jnp.where(allowed, scores, -1e30), axis=2)
    new_max = jnp.maximum(run_max, piece_max)
    expo = jnp.where(allowed, jnp.exp(scores - new_max[:, :, None]), 0.0)
    new_total = jnp.sum(expo, axis=2)
    mixed_values = jnp.einsum(
        "qhk,khd->qhd",
        expo.astype(jnp.bfloat16),
        value_piece.reshape(piece_rows, head_count, HD),
        preferred_element_type=jnp.float32,
    )
    attended = (
        (mixed_values / new_total[:, :, None])
        .astype(jnp.bfloat16)
        .reshape(tok_rows, head_count * HD)
    )
    proj_part = jnp.dot(attended, out_weight, preferred_element_type=jnp.float32)
    share_rows = tok_rows // exp_count
    projected = lax.psum_scatter(
        proj_part.astype(jnp.bfloat16), "exp", scatter_dimension=0, tiled=True
    ).astype(jnp.float32)
    own_residual = lax.dynamic_slice_in_dim(residual, exp_index * share_rows, share_rows, 0).astype(
        jnp.float32
    )
    own_hidden = own_residual + projected
    own_normed = rms_scale(own_hidden, norm_gain).astype(jnp.bfloat16)
    normed = lax.all_gather(own_normed, "exp", axis=0, tiled=True)
    local_experts = gate_weight.shape[0]
    expert_count = local_experts * seq_count
    slot_most = exp_count * max(1, 2 * tok_rows * TOPK // (expert_count * exp_count))
    slot_total = expert_count * slot_most
    pair_count = tok_rows * TOPK
    flat_routes = routes.reshape(pair_count)
    route_onehot = (
        flat_routes[:, None] == jnp.arange(expert_count, dtype=jnp.int32)[None, :]
    ).astype(jnp.int32)
    slot_rank = jnp.sum((jnp.cumsum(route_onehot, axis=0) - 1) * route_onehot, axis=1)
    slot_ids = flat_routes * slot_most + slot_rank
    sources = (
        jnp.full((slot_total,), pair_count, jnp.int32)
        .at[slot_ids]
        .set(jnp.arange(pair_count, dtype=jnp.int32))
    )
    live_slot = sources < pair_count
    token_ids = jnp.minimum(sources, pair_count - 1) // TOPK
    outgoing = jnp.where(live_slot[:, None], normed[token_ids], jnp.zeros((), jnp.bfloat16))
    outgoing = outgoing.reshape(seq_count, local_experts, slot_most, model_width)
    returned = lax.all_to_all(
        expert_block(
            lax.all_to_all(outgoing, "seq", split_axis=0, concat_axis=0, tiled=True),
            gate_weight,
            up_weight,
            down_weight,
        ),
        "seq",
        split_axis=0,
        concat_axis=0,
        tiled=True,
    )
    back_rows = returned.reshape(slot_total, model_width)[slot_ids].astype(jnp.float32)
    weighted = back_rows.reshape(tok_rows, TOPK, model_width) * route_gates[:, :, None]
    mixture_part = jnp.sum(weighted, axis=1)
    own_mixture = lax.psum_scatter(
        mixture_part.astype(jnp.bfloat16), "exp", scatter_dimension=0, tiled=True
    ).astype(jnp.float32)
    return (own_hidden + own_mixture).astype(jnp.bfloat16)


def solution(mesh):
    placed = (
        P("seq", "exp"),
        P("seq", "exp"),
        P("seq", "exp"),
        P("seq", None),
        P("exp", None),
        P(),
        P("seq", None, "exp"),
        P("seq", None, "exp"),
        P("seq", "exp", None),
        P("seq", None),
        P("seq", None),
        P(),
    )
    return jax.shard_map(
        per_device, mesh=mesh, in_specs=placed, out_specs=P(("seq", "exp"), None), check_vma=False
    )
```

profile of v0, /device:TPU:0, one launch (start us, length us, event | category | flops | bytes accessed | tf_op | source)
XLA Modules:
  0.0 345.7 jit_solution(12460206369254408509)
XLA Ops:
  6.5 1.8 copy.47
  8.4 0.0 all-gather.3.cloned.1.call-update
  8.4 0.0 all-gather.5.cloned.1.call-start
  8.4 0.7 all-gather.5.cloned.1.call-update
  9.1 0.0 reduce-scatter.3.cloned.1.call-start
  9.2 0.8 fusion.49
  10.0 0.6 fusion.27
  10.5 0.3 copy.46
  10.8 0.8 copy.53
  11.6 0.1 eq.77
  11.8 1.7 reduce-window.6
  13.5 22.0 %all-gather.3.cloned.1.call-done = bf16[1024,512]{0,1:T(8,128)(2,1)} async-done(((bf16[128,512]{0,1:T(8,128)(2,1)}), bf16[1024,512]{0,1:T(8,128)(2,1)}) %all-gather.3.cloned.1.call-update) | async-done | bytes 1048592 | tf_op jit(solution)/shard_map/all_gather | solution.py:59
  35.4 1.9 fusion.11
  37.3 1.3 copy-done.2
  38.7 0.5 fusion.22
  39.1 21.6 %all-gather.5.cloned.1.call-done = bf16[1024,512]{1,0:T(8,128)(2,1)} async-done(((bf16[128,512]{1,0:T(8,128)(2,1)}), bf16[1024,512]{1,0:T(8,128)(2,1)}) %all-gather.5.cloned.1.call-update) | async-done | bytes 1048592 | tf_op jit(solution)/shard_map/all_gather | solution.py:60
  60.7 2.3 copy.50
  63.0 2.7 fusion.26
  65.8 1.3 convolution_convert_fusion
  67.1 0.0 reduce-scatter.3.cloned.1.call-update
  67.1 0.2 slice_reduce_fusion
  67.3 0.1 eq.73
  67.5 0.1 copy.52
  67.6 0.1 mul.75
  67.8 0.1 fusion.40
  67.9 3.4 scatter_custom_fusion
  71.3 0.1 broadcast_in_dim.60
  71.4 17.6 %reduce-scatter.3.cloned.1.call-done = bf16[32,2048]{1,0:T(8,128)(2,1)} async-done(((bf16[128,2048]{1,0:T(8,128)(2,1)}), bf16[32,2048]{1,0:T(8,128)(2,1)}) %reduce-scatter.3.cloned.1.call-update) | async-done | bytes 131088 | tf_op jit(solution)/shard_map/reduce_scatter | solution.py:93
  89.1 1.1 multiply_reduce_fusion.1
  90.2 1.1 multiply_convert_fusion
  91.3 15.4 %all_gather.11 = bf16[128,2048]{1,0:T(8,128)(2,1)S(1)} all-gather(bf16[32,2048]{1,0:T(8,128)(2,1)S(1)} %multiply_convert_fusion), channel_id=1, replica_groups=mesh['seq'=8,'exp'=4] {'exp'}, dimensions={0}, use_global_device_ids=true | all-gather | bytes 655360 | tf_op jit(solution)/shard_map/all_gather | solution.py:101
  106.6 7.1 %gather_fusion = bf16[1536,2048]{1,0:T(8,128)(2,1)} fusion(bf16[128,2048]{1,0:T(8,128)(2,1)S(1)} %all_gather.11, s32[2048]{0:T(1024)S(1)} %pad_clamp_fusion), kind=kCustom, calls=%fused_computation | custom fusion | bytes 12589056 | tf_op jit(solution)/shard_map/gather | solution.py:120
  113.7 3.3 broadcast_select_fusion
  117.0 75.3 %all_to_all.10 = bf16[8,2,96,2048]{3,2,1,0:T(8,128)(2,1)S(1)} all-to-all(bf16[8,2,96,2048]{3,2,1,0:T(8,128)(2,1)S(1)} %broadcast_select_fusion), channel_id=1, replica_groups=mesh['seq'=8,'exp'=4] {'seq'}, dimensions={0} | all-to-all | bytes 12582912 | tf_op jit(solution)/shard_map/all_to_all | solution.py:124
  192.4 2.7 copy-done.3
  195.0 4.8 %fusion.2 = f32[2,8,96,352]{3,2,1,0:T(8,128)} fusion(bf16[8,2,96,2048]{3,2,1,0:T(8,128)(2,1)S(1)} %all_to_all.10, bf16[2,2048,352]{1,2,0:T(8,128)(2,1)S(1)} %copy-done.9), kind=kOutput, calls=%fused_computation.8 | convolution fusion | flops 2214592512 | bytes 11337728 | tf_op jit(solution)/shard_map/semd,edf->semf/dot_general | solution.py:17
  199.9 11.2 %convert_bitcast_fusion = bf16[8,2,96,2048]{3,2,0,1:T(8,128)(2,1)} fusion(bf16[2,352,2048]{2,1,0:T(8,128)(2,1)S(1)} %copy-done, f32[2,8,96,352]{3,2,1,0:T(8,128)} %fusion.2, bf16[2,2048,352]{1,2,0:T(8,128)(2,1)} %param.19, bf16[8,2,96,2048]{3,2,1,0:T(8,128)(2,1)} %copy-done.3), kind=kOutput, calls=%fused_computation.4 | convolution fusion | flops 4435574784 | bytes 20512768 | tf_op jit(solution)/shard_map/semf,efd->semd/dot_general | solution.py:22
  211.1 6.6 %copy.58 = bf16[8,2,96,2048]{3,2,1,0:T(8,128)(2,1)} copy(bf16[8,2,96,2048]{3,2,0,1:T(8,128)(2,1)} %convert_bitcast_fusion) | data formatting | bytes 12582912 | tf_op jit(solution)/shard_map/convert_element_type | solution.py:24
  217.7 4.9 %all-to-all-start.1 = ((bf16[8,2,96,2048]{3,2,1,0:T(8,128)(2,1)}), bf16[8,2,96,2048]{3,2,1,0:T(8,128)(2,1)}, u32[]{:S(2)}, u32[]{:S(2)}) async-start(bf16[8,2,96,2048]{3,2,1,0:T(8,128)(2,1)} %copy.58), calls=%async_computation.2 | async-start | bytes 12582912 | tf_op jit(solution)/shard_map/all_to_all | solution.py:122
  222.6 0.3 reduce-scatter.5.cloned.1.call-start
  222.8 0.1 copy.59
  223.0 71.2 %all-to-all-done.1 = bf16[8,2,96,2048]{3,2,1,0:T(8,128)(2,1)} async-done(((bf16[8,2,96,2048]{3,2,1,0:T(8,128)(2,1)}), bf16[8,2,96,2048]{3,2,1,0:T(8,128)(2,1)}, u32[]{:S(2)}, u32[]{:S(2)}) %all-to-all-start.1) | async-done | bytes 6291488 | tf_op jit(solution)/shard_map/all_to_all | solution.py:122
  294.1 10.7 %gather_fusion.1 = bf16[768,2048]{1,0:T(8,128)(2,1)} fusion(bf16[1536,2048]{1,0:T(8,128)(2,1)} %bitcast.16, s32[1024]{0:T(1024)S(1)} %pad_clamp_fusion.1), kind=kCustom, calls=%fused_computation.1 | custom fusion | bytes 6294528 | tf_op jit(solution)/shard_map/gather | solution.py:134
  304.8 6.7 %reshape.131 = f32[128,6,2048]{2,1,0:T(8,128)} reshape(bf16[768,2048]{1,0:T(8,128)(2,1)} %gather_fusion.1) | data formatting | bytes 9437184 | tf_op jit(solution)/shard_map/convert_element_type | solution.py:134
  311.5 7.4 %multiply_reduce_fusion = bf16[128,2048]{1,0:T(8,128)(2,1)} fusion(f32[128,6,2048]{2,1,0:T(8,128)} %reshape.131, f32[128,6]{1,0:T(8,128)S(1)} %copy.59), kind=kLoop, calls=%fused_computation.3 | loop fusion | flops 2883584 | bytes 6818816 | tf_op jit(solution)/shard_map/reduce_sum | solution.py:136
  319.0 0.0 reduce-scatter.5.cloned.1.call-update
  319.0 18.5 %reduce-scatter.5.cloned.1.call-done = bf16[32,2048]{1,0:T(8,128)(2,1)} async-done(((bf16[128,2048]{1,0:T(8,128)(2,1)}), bf16[32,2048]{1,0:T(8,128)(2,1)}) %reduce-scatter.5.cloned.1.call-update) | async-done | bytes 131088 | tf_op jit(solution)/shard_map/reduce_scatter | solution.py:137
  337.5 1.7 add_convert_fusion
  (32 shorter events, 0.2 us)
Async XLA Ops:
  6.5 193.3 %copy-start = (bf16[2,352,2048]{2,1,0:T(8,128)(2,1)S(1)}, bf16[2,352,2048]{2,1,0:T(8,128)(2,1)}, u32[]{:S(2)}) copy-start(bf16[2,352,2048]{2,1,0:T(8,128)(2,1)} %param.20) | copy-start | bytes 8650756
  6.5 28.9 %all-gather.3.cloned.1.call-start = ((), (), s32[]{:S(2)}) async-start(), calls=%async_computation.4 | async-start | bytes 1179648 | tf_op jit(solution)/shard_map/all_gather | solution.py:59
  8.4 52.4 %all-gather.5.cloned.1.call-start = ((), (), s32[]{:S(2)}) async-start(), calls=%async_computation.5 | async-start | bytes 1179648 | tf_op jit(solution)/shard_map/all_gather | solution.py:60
  9.1 79.9 %reduce-scatter.3.cloned.1.call-start = ((), (), s32[]{:S(2)}) async-start(), calls=%async_computation.6 | async-start | bytes 655360 | tf_op jit(solution)/shard_map/reduce_scatter | solution.py:93
  37.3 1.4 copy-start.2
  63.0 2.8 copy-start.4
  65.8 1.7 copy-start.6
  65.8 24.4 %copy-start.7 = (f32[2048]{0:T(1024)S(1)}, f32[2048]{0:T(1024)}, u32[]{:S(2)}) copy-start(f32[2048]{0:T(1024)} %param.17) | copy-start | bytes 24580
  117.0 78.0 %copy-start.9 = (bf16[2,2048,352]{1,2,0:T(8,128)(2,1)S(1)}, bf16[2,2048,352]{1,2,0:T(8,128)(2,1)}, u32[]{:S(2)}) copy-start(bf16[2,2048,352]{1,2,0:T(8,128)(2,1)} %param.18) | copy-start | bytes 8650756
  192.4 2.7 copy-start.3
  217.7 5.2 %copy-start.8 = (f32[128,6]{0,1:T(8,128)S(1)}, f32[128,6]{0,1:T(8,128)}, u32[]{:S(2)}) copy-start(f32[128,6]{0,1:T(8,128)} %param.22) | copy-start | bytes 9220
  217.7 76.4 %all-to-all-start.1 = ((bf16[8,2,96,2048]{3,2,1,0:T(8,128)(2,1)}), bf16[8,2,96,2048]{3,2,1,0:T(8,128)(2,1)}, u32[]{:S(2)}, u32[]{:S(2)}) async-start(bf16[8,2,96,2048]{3,2,1,0:T(8,128)(2,1)} %copy.58), calls=%async_computation.2 | async-start | bytes 12582912 | tf_op jit(solution)/shard_map/all_to_all | solution.py:122
  222.6 115.0 %reduce-scatter.5.cloned.1.call-start = ((), (), s32[]{:S(2)}) async-start(), calls=%async_computation.7 | async-start | bytes 655360 | tf_op jit(solution)/shard_map/reduce_scatter | solution.py:137
  304.8 34.4 %copy-start.1 = (bf16[2,352,2048]{2,1,0:T(8,128)(2,1)S(1)}, bf16[2,352,2048]{2,1,0:T(8,128)(2,1)}, u32[]{:S(2)}) copy-start(bf16[2,352,2048]{2,1,0:T(8,128)(2,1)} %param.20) | copy-start | bytes 8650756
  311.5 26.0 %copy-start.5 = (bf16[32,2048]{1,0:T(8,128)(2,1)S(1)}, bf16[32,2048]{1,0:T(8,128)(2,1)}, u32[]{:S(2)}) copy-start(bf16[32,2048]{1,0:T(8,128)(2,1)} %reduce-scatter.3.cloned.1.call-done) | copy-start | bytes 393220
Sparse Core Ops, SparseCore 0:
  9.2 26.1 all-gather.2
  37.3 23.3 all-gather.4
  67.2 21.8 reduce-scatter.2
  319.1 18.3 reduce-scatter.4
where the time goes:
time: 346 us
  waiting for transfers between devices  152 us (44%)
  blocking collectives  90.7 us (26%)
  local copies, waits for them, and re-layouts  44.6 us (13%)
  matrix products  22.5 us (7%)
  other arithmetic  17.8 us (5%)
  between operations  13.3 us (4%)
  starting transfers between devices  5.21 us (2%)
    all_to_all x1, blocking collectives, per_device(): lax.all_to_all(outgoing, 'seq', split_axis=0, concat_axis=0, tiled=True)  75.3 us
    all_to_all x1, waiting for transfers between devices, per_device(): lax.all_to_all(expert_block(lax.all_to_all(outgoing, 'seq', split_axis=0,...  71.2 us
    all_gather x1, waiting for transfers between devices, per_device(): key_piece = lax.all_gather(key_rows, 'seq', axis=0, tiled=True)  22 us
    all_gather x1, waiting for transfers between devices, per_device(): value_piece = lax.all_gather(value_rows, 'seq', axis=0, tiled=True)  21.6 us
    reduce_scatter x1, waiting for transfers between devices, per_device(): lax.psum_scatter(mixture_part.astype(jnp.bfloat16), 'exp', scatter_dimens...  18.5 us
    reduce_scatter x1, waiting for transfers between devices, per_device(): lax.psum_scatter(proj_part.astype(jnp.bfloat16), 'exp', scatter_dimension...  17.6 us
    all_gather x1, blocking collectives, per_device(): normed = lax.all_gather(own_normed, 'exp', axis=0, tiled=True)  15.4 us
    dot_general x1, matrix products, expert_block(): jnp.einsum('semf,efd->semd', inner_act, down_weight, preferred_element_ty...  11.2 us
  transfers between devices with their start and end apart: 5, of which 5 were waited for; matrix products, arithmetic and copies ran while one was open for 3% of the time, Pallas kernels for 0%

commit v1 on v0

--- a/solution.py
+++ b/solution.py
@@ -6,6 +6,12 @@
 HD = 128
 TOPK = 6
 BLK = 512
+
+
+def laid_out(pieces, dim):
+    pieces = jnp.moveaxis(pieces, 0, dim)
+    lengths = pieces.shape
+    return pieces.reshape(*lengths[:dim], lengths[dim] * lengths[dim + 1], *lengths[dim + 2 :])
 
 
 def rms_scale(hidden, norm_gain):
@@ -56,7 +62,19 @@
     split_queries = queries.reshape(tok_rows, head_count, HD)
     score_scale = HD ** (-0.5)
     run_max = jnp.full((tok_rows, head_count), -1e30, jnp.float32)
-    key_piece = lax.all_gather(key_rows, "seq", axis=0, tiled=True)
+    count = lax.axis_size("seq")
+    pairs = [(i, (i + 1) % count) for i in range(count)]
+    back = [(b, a) for a, b in pairs]
+    lower, upper = ([], [])
+    for step in range(count - 1):
+        if step % 2 == 0:
+            lower.append(lax.ppermute(lower[-1] if lower else key_rows, "seq", pairs))
+        else:
+            upper.append(lax.ppermute(upper[-1] if upper else key_rows, "seq", back))
+    blocks = jnp.stack([*lower[::-1], key_rows, *upper])
+    shift = lax.axis_index("seq") - len(lower)
+    blocks = blocks[(jnp.arange(count) - shift) % count]
+    key_piece = laid_out(blocks, 0)
     value_piece = lax.all_gather(value_rows, "seq", axis=0, tiled=True)
     piece_rows = key_piece.shape[0]
     key_pos = jnp.arange(piece_rows, dtype=jnp.int32)

time: 346 us -> 336 us (0.971)
  waiting for transfers between devices: 152 us -> 118 us
  local copies, waits for them, and re-layouts: 44.6 us -> 58.5 us
  starting transfers between devices: 5.21 us -> 14 us
    all_gather x1 -> x0, waiting for transfers between devices: 22 us -> none  [per_device(): key_piece = lax.all_gather(key_rows, 'seq', axis=0, tiled=True)]
    all_gather x1, waiting for transfers between devices: 21.6 us -> 0.02 us  [per_device(): value_piece = lax.all_gather(value_rows, 'seq', axis=0, tiled=True)]
    ppermute x0 -> x7, waiting for transfers between devices: none -> 10.3 us  [the longest x4 10.3 us: per_device(): lower.append(lax.ppermute(lower[-1] if lower else key_rows, 'seq', pairs))]
    ppermute x0 -> x7, starting transfers between devices: none -> 8.81 us  [the longest x3 8.31 us: per_device(): upper.append(lax.ppermute(upper[-1] if upper else key_rows, 'seq', back))]
    unnamed x23 -> x33, local copies, waits for them, and re-layouts: 6.75 us -> 14.1 us
  transfers between devices with their start and end apart: 5 -> 11, of which waited for: 5 -> 6; matrix products, arithmetic and copies ran while one was open for 3% -> 8% of each run, Pallas kernels for 0% -> 0%
where the time goes in v1:
time: 336 us
  waiting for transfers between devices  118 us (35%)
  blocking collectives  90.7 us (27%)
  local copies, waits for them, and re-layouts  58.5 us (17%)
  matrix products  23 us (7%)
  other arithmetic  17.8 us (5%)
  starting transfers between devices  14 us (4%)
  between operations  13.4 us (4%)
    all_to_all x1, blocking collectives, per_device(): lax.all_to_all(outgoing, 'seq', split_axis=0, concat_axis=0, tiled=True)  75.2 us
    all_to_all x1, waiting for transfers between devices, per_device(): lax.all_to_all(expert_block(lax.all_to_all(outgoing, 'seq', split_axis=0,...  71.2 us
    reduce_scatter x1, waiting for transfers between devices, per_device(): lax.psum_scatter(mixture_part.astype(jnp.bfloat16), 'exp', scatter_dimens...  18.5 us
    reduce_scatter x1, waiting for transfers between devices, per_device(): lax.psum_scatter(proj_part.astype(jnp.bfloat16), 'exp', scatter_dimension...  18.2 us
    all_gather x1, blocking collectives, per_device(): normed = lax.all_gather(own_normed, 'exp', axis=0, tiled=True)  15.4 us
    unnamed x33, local copies, waits for them, and re-layouts  14.1 us
    dot_general x1, matrix products, expert_block(): jnp.einsum('semf,efd->semd', inner_act, down_weight, preferred_element_ty...  11.2 us
    gather x1, local copies, waits for them, and re-layouts, per_device(): returned.reshape(slot_total, model_width)[slot_ids].astype(jnp.float32)  10.7 us
  transfers between devices with their start and end apart: 11, of which 6 were waited for; matrix products, arithmetic and copies ran while one was open for 8% of the time, Pallas kernels for 0%

profile of v1, /device:TPU:0, one launch (start us, length us, event | category | flops | bytes accessed | tf_op | source)
XLA Modules:
  0.0 335.6 jit_solution(16027864273944082968)
XLA Ops:
  6.5 0.5 collective-permute-start
  7.0 2.9 collective-permute-start.4
  10.1 0.8 copy.51
  11.0 0.8 fusion.50
  11.8 1.0 collective-permute-done
  12.8 1.2 fusion.27
  14.0 4.2 %collective-permute-done.1 = bf16[128,512]{1,0:T(8,128)(2,1)} collective-permute-done((bf16[128,512]{1,0:T(8,128)(2,1)S(1)}, bf16[128,512]{1,0:T(8,128)(2,1)}, u32[]{:S(2)}, u32[]{:S(2)}) %collective-permute-start.1) | collective-permute-done | bytes 131104 | tf_op jit(solution)/shard_map/ppermute | solution.py:71
  18.2 2.7 collective-permute-start.5
  20.9 5.1 %collective-permute-done.2 = bf16[128,512]{1,0:T(8,128)(2,1)} collective-permute-done((bf16[128,512]{1,0:T(8,128)(2,1)}, bf16[128,512]{1,0:T(8,128)(2,1)}, u32[]{:S(2)}, u32[]{:S(2)}) %collective-permute-start.2) | collective-permute-done | bytes 131104 | tf_op jit(solution)/shard_map/ppermute | solution.py:71
  26.0 1.2 copy.45
  27.2 1.7 reduce-window.6
  28.9 2.7 collective-permute-start.6
  31.6 1.6 bitcast_dynamic-update-slice_fusion.7
  33.2 1.6 bitcast_dynamic-update-slice_fusion.6
  34.8 1.6 bitcast_dynamic-update-slice_fusion.5
  36.3 1.6 bitcast_dynamic-update-slice_fusion.4
  37.9 0.7 bitcast_dynamic-update-slice_fusion.3
  38.6 0.6 bitcast_dynamic-update-slice_fusion.2
  39.2 1.6 bitcast_dynamic-update-slice_fusion.1
  40.8 0.7 bitcast_dynamic-update-slice_fusion
  41.4 2.9 gather_fusion
  44.3 2.2 reshape_reshape.3
  46.5 1.8 fusion.11
  48.2 1.3 copy-done.4
  49.6 0.5 fusion.22
  50.1 2.3 copy.48
  52.4 2.7 fusion.26
  55.1 1.3 convolution_convert_fusion
  57.2 3.4 %scatter_custom_fusion = s32[1536]{0:T(1024)S(1)} fusion(s32[768]{0:T(1024)S(1)} %fusion.52, s32[768]{0:T(1024)S(1)} %iota.41, s32[]{:T(128)} %constant.99.clone.1), kind=kCustom, calls=%fused_computation.85 | custom fusion | bytes 6148 | tf_op jit(solution)/shard_map/scatter | solution.py:134
  60.8 18.2 %reduce-scatter.3.cloned.1.call-done = bf16[32,2048]{1,0:T(8,128)(2,1)} async-done(((bf16[128,2048]{1,0:T(8,128)(2,1)}), bf16[32,2048]{1,0:T(8,128)(2,1)}) %reduce-scatter.3.cloned.1.call-update) | async-done | bytes 131088 | tf_op jit(solution)/shard_map/reduce_scatter | solution.py:111
  79.0 1.1 multiply_reduce_fusion.1
  80.1 1.1 multiply_convert_fusion
  81.2 15.4 %all_gather.7 = bf16[128,2048]{1,0:T(8,128)(2,1)S(1)} all-gather(bf16[32,2048]{1,0:T(8,128)(2,1)S(1)} %multiply_convert_fusion), channel_id=1, replica_groups=mesh['seq'=8,'exp'=4] {'exp'}, dimensions={0}, use_global_device_ids=true | all-gather | bytes 655360 | tf_op jit(solution)/shard_map/all_gather | solution.py:119
  96.6 7.1 %gather_fusion.1 = bf16[1536,2048]{1,0:T(8,128)(2,1)} fusion(bf16[128,2048]{1,0:T(8,128)(2,1)S(1)} %all_gather.7, s32[2048]{0:T(1024)S(1)} %pad_clamp_fusion), kind=kCustom, calls=%fused_computation.1 | custom fusion | bytes 12589056 | tf_op jit(solution)/shard_map/gather | solution.py:138
  103.7 3.3 broadcast_select_fusion
  107.0 75.2 %all_to_all.10 = bf16[8,2,96,2048]{3,2,1,0:T(8,128)(2,1)S(1)} all-to-all(bf16[8,2,96,2048]{3,2,1,0:T(8,128)(2,1)S(1)} %broadcast_select_fusion), channel_id=1, replica_groups=mesh['seq'=8,'exp'=4] {'seq'}, dimensions={0} | all-to-all | bytes 12582912 | tf_op jit(solution)/shard_map/all_to_all | solution.py:142
  182.2 2.7 copy-done.2
  184.9 4.8 %fusion.2 = f32[2,8,96,352]{3,2,1,0:T(8,128)} fusion(bf16[8,2,96,2048]{3,2,1,0:T(8,128)(2,1)S(1)} %all_to_all.10, bf16[2,2048,352]{1,2,0:T(8,128)(2,1)S(1)} %copy-done.11), kind=kOutput, calls=%fused_computation.9 | convolution fusion | flops 2214592512 | bytes 11337728 | tf_op jit(solution)/shard_map/semd,edf->semf/dot_general | solution.py:23
  189.8 11.2 %convert_bitcast_fusion = bf16[8,2,96,2048]{3,2,0,1:T(8,128)(2,1)} fusion(bf16[2,352,2048]{2,1,0:T(8,128)(2,1)S(1)} %copy-done, f32[2,8,96,352]{3,2,1,0:T(8,128)} %fusion.2, bf16[2,2048,352]{1,2,0:T(8,128)(2,1)} %param.19, bf16[8,2,96,2048]{3,2,1,0:T(8,128)(2,1)} %copy-done.2), kind=kOutput, calls=%fused_computation.5 | convolution fusion | flops 4435574784 | bytes 20512768 | tf_op jit(solution)/shard_map/semf,efd->semd/dot_general | solution.py:28
  201.0 6.6 %copy.56 = bf16[8,2,96,2048]{3,2,1,0:T(8,128)(2,1)} copy(bf16[8,2,96,2048]{3,2,0,1:T(8,128)(2,1)} %convert_bitcast_fusion) | data formatting | bytes 12582912 | tf_op jit(solution)/shard_map/convert_element_type | solution.py:30
  207.6 4.9 %all-to-all-start.1 = ((bf16[8,2,96,2048]{3,2,1,0:T(8,128)(2,1)}), bf16[8,2,96,2048]{3,2,1,0:T(8,128)(2,1)}, u32[]{:S(2)}, u32[]{:S(2)}) async-start(bf16[8,2,96,2048]{3,2,1,0:T(8,128)(2,1)} %copy.56), calls=%async_computation.2 | async-start | bytes 12582912 | tf_op jit(solution)/shard_map/all_to_all | solution.py:140
  212.4 0.3 reduce-scatter.5.cloned.1.call-start
  212.8 71.2 %all-to-all-done.1 = bf16[8,2,96,2048]{3,2,1,0:T(8,128)(2,1)} async-done(((bf16[8,2,96,2048]{3,2,1,0:T(8,128)(2,1)}), bf16[8,2,96,2048]{3,2,1,0:T(8,128)(2,1)}, u32[]{:S(2)}, u32[]{:S(2)}) %all-to-all-start.1) | async-done | bytes 6291488 | tf_op jit(solution)/shard_map/all_to_all | solution.py:140
  284.0 10.7 %gather_fusion.2 = bf16[768,2048]{1,0:T(8,128)(2,1)} fusion(bf16[1536,2048]{1,0:T(8,128)(2,1)} %bitcast.24, s32[1024]{0:T(1024)S(1)} %pad_clamp_fusion.1), kind=kCustom, calls=%fused_computation.2 | custom fusion | bytes 6294528 | tf_op jit(solution)/shard_map/gather | solution.py:152
  294.7 6.7 %reshape.176 = f32[128,6,2048]{2,1,0:T(8,128)} reshape(bf16[768,2048]{1,0:T(8,128)(2,1)} %gather_fusion.2) | data formatting | bytes 9437184 | tf_op jit(solution)/shard_map/convert_element_type | solution.py:152
  301.4 7.4 %multiply_reduce_fusion = bf16[128,2048]{1,0:T(8,128)(2,1)} fusion(f32[128,6,2048]{2,1,0:T(8,128)} %reshape.176, f32[128,6]{1,0:T(8,128)S(1)} %copy.57), kind=kLoop, calls=%fused_computation.4 | loop fusion | flops 2883584 | bytes 6818816 | tf_op jit(solution)/shard_map/reduce_sum | solution.py:154
  308.9 18.5 %reduce-scatter.5.cloned.1.call-done = bf16[32,2048]{1,0:T(8,128)(2,1)} async-done(((bf16[128,2048]{1,0:T(8,128)(2,1)}), bf16[32,2048]{1,0:T(8,128)(2,1)}) %reduce-scatter.5.cloned.1.call-update) | async-done | bytes 131088 | tf_op jit(solution)/shard_map/reduce_scatter | solution.py:155
  327.4 1.7 add_convert_fusion
  (58 shorter events, 1.4 us)
Async XLA Ops:
  6.5 183.2 %copy-start = (bf16[2,352,2048]{2,1,0:T(8,128)(2,1)S(1)}, bf16[2,352,2048]{2,1,0:T(8,128)(2,1)}, u32[]{:S(2)}) copy-start(bf16[2,352,2048]{2,1,0:T(8,128)(2,1)} %param.20) | copy-start | bytes 8650756
  6.5 31.4 %copy-start.6 = (bf16[128,512]{1,0:T(8,128)(2,1)S(1)}, bf16[128,512]{1,0:T(8,128)(2,1)}, u32[]{:S(2)}) copy-start(bf16[128,512]{1,0:T(8,128)(2,1)} %param.13) | copy-start | bytes 393220
  6.5 43.5 %all-gather.2.cloned.1.call-start = ((), (), s32[]{:S(2)}) async-start(), calls=%async_computation.4 | async-start | bytes 1179648 | tf_op jit(solution)/shard_map/all_gather | solution.py:78
  6.5 6.3 %collective-permute-start = (bf16[128,512]{1,0:T(8,128)(2,1)}, bf16[128,512]{1,0:T(8,128)(2,1)S(1)}, u32[]{:S(2)}, u32[]{:S(2)}) collective-permute-start(bf16[128,512]{1,0:T(8,128)(2,1)} %param.13), channel_id=1, source_target_pairs={{0,4},{4,8},{8,12},{12,16},{16,20},{20,24},{24,28},{28,0},{1,5},{5... | collective-permute-start | bytes 393224 | tf_op jit(solution)/shard_map/ppermute | solution.py:71
  7.0 11.2 %collective-permute-start.4 = (bf16[128,512]{1,0:T(8,128)(2,1)}, bf16[128,512]{1,0:T(8,128)(2,1)S(1)}, u32[]{:S(2)}, u32[]{:S(2)}) collective-permute-start(bf16[128,512]{1,0:T(8,128)(2,1)} %param.13), channel_id=1, source_target_pairs={{4,0},{8,4},{12,8},{16,12},{20,16},{24,20},{28,24},{0,28},{5,1},{9... | collective-permute-start | bytes 393224 | tf_op jit(solution)/shard_map/ppermute | solution.py:73
  10.0 69.0 %reduce-scatter.3.cloned.1.call-start = ((), (), s32[]{:S(2)}) async-start(), calls=%async_computation.5 | async-start | bytes 655360 | tf_op jit(solution)/shard_map/reduce_scatter | solution.py:111
  12.8 13.2 %copy-start.7 = (bf16[128,512]{1,0:T(8,128)(2,1)}, bf16[128,512]{1,0:T(8,128)(2,1)S(1)}, u32[]{:S(2)}) copy-start(bf16[128,512]{1,0:T(8,128)(2,1)S(1)} %collective-permute-done) | copy-start | bytes 393220
  12.8 5.4 %collective-permute-start.1 = (bf16[128,512]{1,0:T(8,128)(2,1)S(1)}, bf16[128,512]{1,0:T(8,128)(2,1)}, u32[]{:S(2)}, u32[]{:S(2)}) collective-permute-start(bf16[128,512]{1,0:T(8,128)(2,1)S(1)} %collective-permute-done), channel_id=1, source_target_pairs={{0,4},{4,8},{8,12},{12,16},{16,20},{20,24},{24,28},{28,0},{1,5},{5... | collective-permute-start | bytes 393224 | tf_op jit(solution)/shard_map/ppermute | solution.py:71
  18.2 7.8 %collective-permute-start.2 = (bf16[128,512]{1,0:T(8,128)(2,1)}, bf16[128,512]{1,0:T(8,128)(2,1)}, u32[]{:S(2)}, u32[]{:S(2)}) collective-permute-start(bf16[128,512]{1,0:T(8,128)(2,1)} %collective-permute-done.1), channel_id=1, source_target_pairs={{0,4},{4,8},{8,12},{12,16},{16,20},{20,24},{24,28},{28,0},{1,5},{5... | collective-permute-start | bytes 393224 | tf_op jit(solution)/shard_map/ppermute | solution.py:71
  18.2 10.7 %collective-permute-start.5 = (bf16[128,512]{1,0:T(8,128)(2,1)S(1)}, bf16[128,512]{1,0:T(8,128)(2,1)}, u32[]{:S(2)}, u32[]{:S(2)}) collective-permute-start(bf16[128,512]{1,0:T(8,128)(2,1)S(1)} %collective-permute-done.4), channel_id=1, source_target_pairs={{4,0},{8,4},{12,8},{16,12},{20,16},{24,20},{28,24},{0,28},{5,1},{9... | collective-permute-start | bytes 393224 | tf_op jit(solution)/shard_map/ppermute | solution.py:73
  26.0 5.6 %collective-permute-start.3 = (bf16[128,512]{1,0:T(8,128)(2,1)}, bf16[128,512]{1,0:T(8,128)(2,1)}, u32[]{:S(2)}, u32[]{:S(2)}) collective-permute-start(bf16[128,512]{1,0:T(8,128)(2,1)} %collective-permute-done.2), channel_id=1, source_target_pairs={{0,4},{4,8},{8,12},{12,16},{16,20},{20,24},{24,28},{28,0},{1,5},{5... | collective-permute-start | bytes 393224 | tf_op jit(solution)/shard_map/ppermute | solution.py:71
  28.9 11.8 %collective-permute-start.6 = (bf16[128,512]{1,0:T(8,128)(2,1)}, bf16[128,512]{1,0:T(8,128)(2,1)S(1)}, u32[]{:S(2)}, u32[]{:S(2)}) collective-permute-start(bf16[128,512]{1,0:T(8,128)(2,1)} %collective-permute-done.5), channel_id=1, source_target_pairs={{4,0},{8,4},{12,8},{16,12},{20,16},{24,20},{28,24},{0,28},{5,1},{9... | collective-permute-start | bytes 393224 | tf_op jit(solution)/shard_map/ppermute | solution.py:73
  48.2 1.4 copy-start.4
  52.4 2.8 copy-start.3
  55.1 1.7 copy-start.8
  55.1 25.0 %copy-start.9 = (f32[2048]{0:T(1024)S(1)}, f32[2048]{0:T(1024)}, u32[]{:S(2)}) copy-start(f32[2048]{0:T(1024)} %param.17) | copy-start | bytes 24580
  107.0 77.9 %copy-start.11 = (bf16[2,2048,352]{1,2,0:T(8,128)(2,1)S(1)}, bf16[2,2048,352]{1,2,0:T(8,128)(2,1)}, u32[]{:S(2)}) copy-start(bf16[2,2048,352]{1,2,0:T(8,128)(2,1)} %param.18) | copy-start | bytes 8650756
  182.2 2.7 copy-start.2
  207.6 5.2 %copy-start.10 = (f32[128,6]{0,1:T(8,128)S(1)}, f32[128,6]{0,1:T(8,128)}, u32[]{:S(2)}) copy-start(f32[128,6]{0,1:T(8,128)} %param.22) | copy-start | bytes 9220
  207.6 76.4 %all-to-all-start.1 = ((bf16[8,2,96,2048]{3,2,1,0:T(8,128)(2,1)}), bf16[8,2,96,2048]{3,2,1,0:T(8,128)(2,1)}, u32[]{:S(2)}, u32[]{:S(2)}) async-start(bf16[8,2,96,2048]{3,2,1,0:T(8,128)(2,1)} %copy.56), calls=%async_computation.2 | async-start | bytes 12582912 | tf_op jit(solution)/shard_map/all_to_all | solution.py:140
  212.4 115.0 %reduce-scatter.5.cloned.1.call-start = ((), (), s32[]{:S(2)}) async-start(), calls=%async_computation.6 | async-start | bytes 655360 | tf_op jit(solution)/shard_map/reduce_scatter | solution.py:155
  294.7 34.4 %copy-start.1 = (bf16[2,352,2048]{2,1,0:T(8,128)(2,1)S(1)}, bf16[2,352,2048]{2,1,0:T(8,128)(2,1)}, u32[]{:S(2)}) copy-start(bf16[2,352,2048]{2,1,0:T(8,128)(2,1)} %param.20) | copy-start | bytes 8650756
  301.4 26.0 %copy-start.5 = (bf16[32,2048]{1,0:T(8,128)(2,1)S(1)}, bf16[32,2048]{1,0:T(8,128)(2,1)}, u32[]{:S(2)}) copy-start(bf16[32,2048]{1,0:T(8,128)(2,1)} %reduce-scatter.3.cloned.1.call-done) | copy-start | bytes 393220
Sparse Core Ops, SparseCore 0:
  10.1 27.6 all-gather.1
  56.5 22.3 reduce-scatter.2
  309.0 18.3 reduce-scatter.4
